TPU v7x, 32 devices: a whole 2x2x4 slice. The times are simulated.
32 devices in a mesh: dp: 8 (over y, x, core), replica: 4 (over z).
Axes of the slice: x: 2, y: 2, z: 4, core: 2. Of those that a mesh axis runs over, the one named last changes fastest.
Arguments:
- gradient: bfloat16 [4, 8, 8, 8192], P('replica', 'dp'), may hold values from -6 to 6
- master: float32 [8, 8192], P('dp', 'replica'), may hold values from -0.0625 to 0.0625
- moment: float32 [8, 8192], P('dp', 'replica'), may hold values from -0.046875 to 0.046875
- second: float32 [8, 8192], P('dp', 'replica'), may hold values from 1e-06 to 0.0001
Outputs:
- new_params: bfloat16 [8, 8192], P('dp')
- new_master: float32 [8, 8192], P('dp', 'replica')
- new_moment: float32 [8, 8192], P('dp', 'replica')
- new_second: float32 [8, 8192], P('dp', 'replica')
- direction: float32 [8, 8192], P('dp', 'replica')
- ratios: float32 [4], replicated
All inputs are finite; a program needn't handle non-finite values.
Results may differ from a plain program's by a relative error of at most 0.001.
Values may be sent and summed in bfloat16 or wider, within the bound.
A program may use at most 64 MiB of HBM per device.

v0:
```python
import jax
import jax.numpy as jnp
from jax import lax
from jax.sharding import PartitionSpec as P

MATS = 4
STEP = 2


def local(gradient, master, moment, second):
    raw_rows = gradient[0, 0]
    rows_all, width = raw_rows.shape
    data_count = lax.axis_size("dp")
    rep_count = lax.axis_size("replica")
    row_dev = rows_all // data_count
    terms = raw_rows.astype(jnp.float32)
    owned_rows = lax.psum_scatter(terms, "dp", scatter_dimension=0, tiled=True)
    summed = lax.psum_scatter(owned_rows, "replica", scatter_dimension=1, tiled=True)
    grad = summed / (data_count * rep_count)
    new_moment = 0.9 * moment + 0.1 * grad
    new_second = 0.999 * second + 0.001 * grad * grad
    first_fix = 1.0 - 0.9**STEP
    second_fix = 1.0 - 0.999**STEP
    direction = new_moment / first_fix / (jnp.sqrt(new_second / second_fix) + 1e-08)
    new_master = master - 0.0003 * (direction + 0.1 * master)
    row_ids = lax.axis_index("dp") * row_dev + lax.iota(jnp.int32, row_dev)
    owner_mat = row_ids // (rows_all // MATS)
    member = (owner_mat[:, None] == lax.iota(jnp.int32, MATS)[None, :]).astype(jnp.float32)
    dir_rows = jnp.sum(direction * direction, axis=1)
    wgt_rows = jnp.sum(master * master, axis=1)
    dir_part = jnp.sum(member * dir_rows[:, None], axis=0)
    wgt_part = jnp.sum(member * wgt_rows[:, None], axis=0)
    dir_sq, wgt_sq = lax.psum((dir_part, wgt_part), ("dp", "replica"))
    ratios = jnp.sqrt(dir_sq) / (jnp.sqrt(wgt_sq) + 1e-06)
    new_params = lax.all_gather(new_master.astype(jnp.bfloat16), "replica", axis=1, tiled=True)
    return (new_params, new_master, new_moment, new_second, direction, ratios)


def solution(mesh):
    return jax.shard_map(
        local,
        mesh=mesh,
        in_specs=(
            P("replica", "dp", None, None),
            P("dp", "replica"),
            P("dp", "replica"),
            P("dp", "replica"),
        ),
        out_specs=(
            P("dp", None),
            P("dp", "replica"),
            P("dp", "replica"),
            P("dp", "replica"),
            P("dp", "replica"),
            P(),
        ),
        check_vma=False,
    )
```

profile of v0, /device:TPU:0, one launch (start us, length us, event | category | flops | bytes accessed | tf_op | source)
XLA Modules:
  0.0 214.0 jit_solution(4225715408327386011)
XLA Ops:
  7.2 0.0 all-reduce.4.cloned.1.call-start
  7.2 1.6 bitcast_convert_fusion
  8.8 0.0 all-reduce.4.cloned.1.call-update
  8.9 0.0 reduce-scatter.4.cloned.1.call-start
  8.9 1.2 dynamic-slice
  10.2 57.2 %all-reduce.4.cloned.1.call-done = f32[8,8192]{1,0:T(8,128)} async-done(((f32[8,8192]{1,0:T(8,128)}), f32[8,8192]{1,0:T(8,128)}) %all-reduce.4.cloned.1.call-update) | async-done | bytes 262160
  67.3 1.6 constant_dynamic-slice_fusion
  68.9 0.0 copy-start.1
  69.0 0.0 copy-start.2
  69.0 0.0 copy-start.3
  69.0 2.6 %copy.10 = f32[1,8192]{0,1:T(8,128)} copy(f32[1,8192]{1,0:T(1,128)S(1)} %constant_dynamic-slice_fusion) | data formatting | bytes 65536
  71.6 0.0 reduce-scatter.4.cloned.1.call-update
  71.6 76.3 %reduce-scatter.4.cloned.1.call-done = f32[2048,1]{1,0:T(8,128)} async-done(((f32[8192,1]{1,0:T(8,128)}), f32[2048,1]{1,0:T(8,128)}) %reduce-scatter.4.cloned.1.call-update) | async-done | bytes 8208
  147.9 1.6 copy.11
  149.5 0.0 copy-done.1
  149.5 0.0 copy-done.2
  149.5 1.3 multiply_reduce_fusion.1
  150.7 0.0 copy-start
  150.7 0.0 copy-done.3
  150.7 1.2 fusion
  152.0 13.7 %all_gather.3 = bf16[1,8192]{1,0:T(2,128)(2,1)S(1)} all-gather(bf16[1,2048]{1,0:T(2,128)(2,1)S(1)} %get-tuple-element.12), channel_id=1, replica_groups=mesh['dp'=8,'replica'=4] {'replica'}, dimensions={1}, use_global_device_ids=true | all-gather | bytes 20480 | tf_op jit(solution)/shard_map/all_gather | solution.py:35
  165.6 1.3 compare_select_fusion
  166.9 39.1 %all-reduce.1 = (f32[4]{0:T(128)S(1)}, f32[4]{0:T(128)S(1)}) all-reduce(f32[4]{0:T(128)S(1)} %get-tuple-element.15, f32[4]{0:T(128)S(1)} %get-tuple-element.16), channel_id=1, replica_groups=mesh['dp'=8,'replica'=4] {'dp','replica'}, use_global_device_ids=true, to_apply=%region_5.6 | all-reduce | flops 8 | bytes 64 | tf_op jit(solution)/shard_map/psum | solution.py:33
  206.0 0.5 add_divide_fusion.1
  206.6 0.6 copy.14
  207.2 0.0 copy-done
Async XLA Ops:
  7.2 60.1 %all-reduce.4.cloned.1.call-start = ((), (), s32[]{:S(2)}) async-start(), calls=%async_computation.2 | async-start | bytes 524288
  8.9 139.1 %reduce-scatter.4.cloned.1.call-start = ((), (), s32[]{:S(2)}) async-start(), calls=%async_computation.1 | async-start | bytes 5242880
  68.9 80.5 %copy-start.1 = (f32[1,2048]{1,0:T(1,128)S(1)}, f32[1,2048]{1,0:T(1,128)}, u32[]{:S(2)}) copy-start(f32[1,2048]{1,0:T(1,128)} %param.6) | copy-start | bytes 24580
  69.0 80.5 %copy-start.2 = (f32[1,2048]{1,0:T(1,128)S(1)}, f32[1,2048]{1,0:T(1,128)}, u32[]{:S(2)}) copy-start(f32[1,2048]{1,0:T(1,128)} %param.7) | copy-start | bytes 24580
  69.0 81.8 %copy-start.3 = (f32[1,2048]{1,0:T(1,128)S(1)}, f32[1,2048]{1,0:T(1,128)}, u32[]{:S(2)}) copy-start(f32[1,2048]{1,0:T(1,128)} %param.5) | copy-start | bytes 24580
  150.7 56.4 %copy-start = (f32[1,2048]{1,0:T(1,128)}, f32[1,2048]{1,0:T(1,128)S(1)}, u32[]{:S(2)}) copy-start(f32[1,2048]{1,0:T(1,128)S(1)} %get-tuple-element.27) | copy-start | bytes 24580
Sparse Core Ops, SparseCore 0:
  11.1 56.2 all-reduce.3
  71.7 76.1 reduce-scatter.3
where the time goes:
time: 214 us
  waiting for transfers between devices  133 us (62%)
  blocking collectives  52.8 us (25%)
  between operations  14.1 us (7%)
  local copies, waits for them, and re-layouts  7.67 us (4%)
  other arithmetic  5.92 us (3%)
    unnamed x4, waiting for transfers between devices  133 us
    psum x1, blocking collectives, local(): dir_sq, wgt_sq = lax.psum((dir_part, wgt_part), ('dp', 'replica'))  39.1 us
    all_gather x1, blocking collectives, local(): lax.all_gather(new_master.astype(jnp.bfloat16), 'replica', axis=1, tiled=...  13.7 us
    unnamed x13, local copies, waits for them, and re-layouts  7.67 us
  transfers between devices with their start and end apart: 2, of which 2 were waited for; matrix products, arithmetic and copies ran while one was open for 1% of the time, Pallas kernels for 0%

commit v1 on v0

v1 whole, which is shorter than its diff:
```python
import functools

import jax
import jax.numpy as jnp
from jax import lax
from jax.experimental import pallas as pl
from jax.experimental.pallas import tpu as pltpu
from jax.sharding import PartitionSpec as P

MATS = 4
STEP = 2
LANES = 128
IDS = pl.DeviceIdType.MESH


def kernel(n_dp, n_rep, grad_hbm, master_hbm, moment_hbm, second_hbm,
           row_out, master_out, moment_out, second_out, dir_out, ratio_out,
           raw, state, tiles, rows_out, rows_in, parts, full, stats,
           load_sem, state_send, state_recv, row_send, row_recv,
           part_send, part_recv, stat_send, stat_recv):
    dp = lax.axis_index("dp")
    rep = lax.axis_index("replica")
    rows, width = raw.shape
    length = width // LANES
    block = length // n_rep

    def dp_peer(k):
        return {"dp": lax.rem(dp + k, n_dp)}

    def rep_peer(k):
        return {"replica": lax.rem(rep + k, n_rep)}

    def remote(src, dst, send, recv, peer):
        return pltpu.make_async_remote_copy(
            src_ref=src, dst_ref=dst, send_sem=send, recv_sem=recv,
            device_id=peer, device_id_type=IDS)

    own = pl.ds(pl.multiple_of(rep * block, block), block)
    grad_load = pltpu.make_async_copy(grad_hbm, raw, load_sem.at[0])
    grad_load.start()
    state_loads = [
        pltpu.make_async_copy(ref, state.at[i, own], load_sem.at[1 + i])
        for i, ref in enumerate((master_hbm, moment_hbm, second_hbm))
    ]
    for load in state_loads:
        load.start()

    barrier = pltpu.get_barrier_semaphore()
    for k in range(1, n_dp):
        pl.semaphore_signal(barrier, inc=1, device_id=dp_peer(k), device_id_type=IDS)
    for k in range(1, n_rep):
        pl.semaphore_signal(barrier, inc=1, device_id=rep_peer(k), device_id_type=IDS)

    grad_load.wait()
    for t in range(length):
        tile = raw[:, t * LANES:(t + 1) * LANES].astype(jnp.float32)
        tiles[t * rows:(t + 1) * rows, :] = tile
    pl.semaphore_wait(barrier, n_dp + n_rep - 2)

    row_copies = []
    for k in range(1, n_dp):
        peer = lax.rem(dp + k, n_dp)
        rows_out[k] = tiles[pl.ds(peer, length, stride=rows), :].astype(jnp.bfloat16)
        copy = remote(rows_out.at[k], rows_in.at[k], row_send.at[k], row_recv.at[k], dp_peer(k))
        copy.start()
        row_copies.append(copy)

    for load in state_loads:
        load.wait()
    state_copies = []
    for k in range(1, n_rep):
        copy = remote(state.at[:, own], state.at[:, own], state_send.at[k], state_recv.at[k], rep_peer(k))
        copy.start()
        state_copies.append(copy)

    total = tiles[pl.ds(dp, length, stride=rows), :]
    for k in range(1, n_dp):
        row_copies[k - 1].wait_recv()
        total = total + rows_in[k].astype(jnp.float32)
    parts[rep] = total
    part_copies = []
    for k in range(1, n_rep):
        copy = remote(parts.at[rep], parts.at[rep], part_send.at[k], part_recv.at[k], rep_peer(k))
        copy.start()
        part_copies.append(copy)

    for copy in state_copies:
        copy.wait_recv()
    for copy in part_copies:
        copy.wait_recv()
    summed = parts[0]
    for r in range(1, n_rep):
        summed = summed + parts[r]
    grad = summed / (n_dp * n_rep)
    master = state[0]
    new_moment = 0.9 * state[1] + 0.1 * grad
    new_second = 0.999 * state[2] + 0.001 * grad * grad
    first_fix = 1.0 - 0.9**STEP
    second_fix = 1.0 - 0.999**STEP
    direction = new_moment / first_fix / (jnp.sqrt(new_second / second_fix) + 1e-08)
    dir_sq = jnp.sum(direction * direction, axis=0, keepdims=True)
    wgt_sq = jnp.sum(master * master, axis=0, keepdims=True)
    stats[dp] = jnp.concatenate([dir_sq, wgt_sq], axis=0)
    stat_copies = []
    for k in range(1, n_dp):
        copy = remote(stats.at[dp], stats.at[dp], stat_send.at[k], stat_recv.at[k], dp_peer(k))
        copy.start()
        stat_copies.append(copy)

    new_master = master - 0.0003 * (direction + 0.1 * master)
    row_out[...] = new_master
    for i, value in enumerate((new_master, new_moment, new_second, direction)):
        full[i] = value
    for i, out in enumerate((master_out, moment_out, second_out, dir_out)):
        out[...] = full[i, own]

    for copy in stat_copies:
        copy.wait_recv()
    per_mat = rows // MATS
    lane = lax.broadcasted_iota(jnp.int32, (1, LANES), 1)
    ratios = jnp.zeros((1, LANES), jnp.float32)
    for m in range(MATS):
        pair = stats[m * per_mat]
        for r in range(1, per_mat):
            pair = pair + stats[m * per_mat + r]
        norms = jnp.sqrt(jnp.sum(pair, axis=1, keepdims=True))
        ratio = norms[0:1] / (norms[1:2] + 1e-06)
        ratios = jnp.where(lane == m, ratio, ratios)
    ratio_out[...] = ratios

    for copy in row_copies + state_copies + part_copies + stat_copies:
        copy.wait_send()


def local(gradient, master, moment, second):
    raw_rows = gradient[0, 0]
    rows, width = raw_rows.shape
    n_dp = lax.axis_size("dp")
    n_rep = lax.axis_size("replica")
    cols = master.shape[1]
    length, block = width // LANES, cols // LANES
    f32 = jnp.float32
    vmem = pl.BlockSpec(memory_space=pltpu.VMEM)
    dma = pltpu.SemaphoreType.DMA
    flat = [a.reshape(block, LANES) for a in (master, moment, second)]
    outs = pl.pallas_call(
        functools.partial(kernel, n_dp, n_rep),
        out_shape=[jax.ShapeDtypeStruct((length, LANES), f32)]
        + [jax.ShapeDtypeStruct((block, LANES), f32)] * 4
        + [jax.ShapeDtypeStruct((1, LANES), f32)],
        in_specs=[pl.BlockSpec(memory_space=pl.ANY)] * 4,
        out_specs=[vmem] * 6,
        scratch_shapes=[
            pltpu.VMEM((rows, width), jnp.bfloat16),
            pltpu.VMEM((3, length, LANES), f32),
            pltpu.VMEM((rows * length, LANES), f32),
            pltpu.VMEM((n_dp, length, LANES), jnp.bfloat16),
            pltpu.VMEM((n_dp, length, LANES), jnp.bfloat16),
            pltpu.VMEM((n_rep, length, LANES), f32),
            pltpu.VMEM((4, length, LANES), f32),
            pltpu.VMEM((n_dp, 2, LANES), f32),
            dma((4,)),
            dma((n_rep,)), dma((n_rep,)),
            dma((n_dp,)), dma((n_dp,)),
            dma((n_rep,)), dma((n_rep,)),
            dma((n_dp,)), dma((n_dp,)),
        ],
        compiler_params=pltpu.CompilerParams(collective_id=0, has_side_effects=True),
    )(raw_rows, *flat)
    row, new_master, new_moment, new_second, direction, ratios = outs
    new_params = row.reshape(1, width).astype(jnp.bfloat16)
    blocks = [a.reshape(1, cols) for a in (new_master, new_moment, new_second, direction)]
    return (new_params, *blocks, ratios[0, :MATS])


def solution(mesh):
    return jax.shard_map(
        local,
        mesh=mesh,
        in_specs=(
            P("replica", "dp", None, None),
            P("dp", "replica"),
            P("dp", "replica"),
            P("dp", "replica"),
        ),
        out_specs=(
            P("dp", None),
            P("dp", "replica"),
            P("dp", "replica"),
            P("dp", "replica"),
            P("dp", "replica"),
            P(),
        ),
        check_vma=False,
    )
```

time: 214 us -> 24.2 us (0.11)
  waiting for transfers between devices: 133 us -> 0 us
  blocking collectives: 52.8 us -> 0 us
  Pallas kernels: 0 us -> 17.8 us
  between operations: 14.1 us -> 0.65 us
  other arithmetic: 5.92 us -> 0.76 us
  local copies, waits for them, and re-layouts: 7.67 us -> 4.57 us
    unnamed x4 -> x0, waiting for transfers between devices: 133 us -> none
    psum x1 -> x0, blocking collectives: 39.1 us -> none  [local(): dir_sq, wgt_sq = lax.psum((dir_part, wgt_part), ('dp', 'replica'))]
    pallas_call x0 -> x1, Pallas kernels: none -> 17.8 us  [local(): pl.pallas_call(functools.partial(kernel, n_dp, n_rep), out_shape=[jax.Sha...]
    all_gather x1 -> x0, blocking collectives: 13.7 us -> none  [local(): lax.all_gather(new_master.astype(jnp.bfloat16), 'replica', axis=1, tiled=...]
    unnamed x13 -> x15, local copies, waits for them, and re-layouts: 7.67 us -> 4.06 us
    convert_element_type x2 -> x0, other arithmetic: 2.84 us -> none  [the longest x1 1.62 us: local(): terms = raw_rows.astype(jnp.float32)]
  transfers between devices with their start and end apart: 2 -> 0, of which waited for: 2 -> 0; matrix products, arithmetic and copies ran while one was open for 1% -> 0% of each run, Pallas kernels for 0% -> 0%
where the time goes in v1:
time: 24.2 us; the launch traced here: 23.8 us
  Pallas kernels  17.8 us (74%)
  local copies, waits for them, and re-layouts  4.57 us (19%)
  other arithmetic  0.76 us (3%)
  between operations  0.65 us (3%)
    pallas_call x1, Pallas kernels, local(): pl.pallas_call(functools.partial(kernel, n_dp, n_rep), out_shape=[jax.Sha...  17.8 us
    unnamed x15, local copies, waits for them, and re-layouts  4.06 us
    unnamed x1, other arithmetic  0.76 us
    squeeze x1, local copies, waits for them, and re-layouts, local(): return (new_params, *blocks, ratios[0, :MATS])  0.51 us

profile of v1, /device:TPU:0, one launch (start us, length us, event | category | flops | bytes accessed | tf_op | source)
XLA Modules:
  0.0 23.8 jit_solution(6790656857772226229)
XLA Ops:
  0.6 17.8 %shard_map.91 = (f32[64,128]{1,0:T(8,128)}, f32[16,128]{1,0:T(8,128)}, f32[16,128]{1,0:T(8,128)}, f32[16,128]{1,0:T(8,128)}, f32[16,128]{1,0:T(8,128)}, /*index=5*/f32[1,128]{1,0:T(1,128)}) custom-call(bf16[8,8192]{1,0:T(8,128)(2,1)} %bitcast.16, f32[16,128]{1,0:T(8,128)} %bitcast.18, f32[16,128]{1,0:T(8,128)} %bitcast.19, f32[16,128]{1,0:T(8,128)} %bitcast.20), custom_call_target="tpu_custom_call" | custom-call | tf_op jit(solution)/shard_map/pallas_call | solution.py:146
  18.5 0.8 %convert_bitcast_fusion = bf16[1,1,64,128]{3,2,1,0:T(8,128)(2,1)S(1)} fusion(f32[64,128]{1,0:T(8,128)} %get-tuple-element.12), kind=kLoop, calls=%fused_computation.1 | loop fusion | flops 8192 | bytes 49152
  19.2 0.0 copy-start.4
  19.2 0.7 %copy-done.4 = f32[1,128]{1,0:T(1,128)S(1)} copy-done((f32[1,128]{1,0:T(1,128)S(1)}, f32[1,128]{1,0:T(1,128)}, u32[]{:S(2)}) %copy-start.4) | copy-done | bytes 536
  19.9 0.5 %slice_bitcast_fusion = f32[4]{0:T(128)} fusion(f32[1,128]{1,0:T(1,128)S(1)} %copy-done.4), kind=kLoop, calls=%fused_computation.2 | loop fusion | bytes 32 | tf_op jit(solution)/shard_map/squeeze | solution.py:173
  20.4 0.0 copy-start.3
  20.4 0.6 %copy.12 = bf16[1,1,64,128]{3,1,2,0:T(2,128)(2,1)} copy(bf16[1,1,64,128]{3,2,1,0:T(8,128)(2,1)S(1)} %convert_bitcast_fusion) | data formatting | bytes 32768
  21.0 0.1 copy-done.3
  21.1 0.0 copy-start.2
  21.1 0.6 %copy.17 = f32[1,2048]{1,0:T(1,128)} copy(f32[1,2048]{1,0:T(1,128)S(1)} %bitcast.24) | data formatting | bytes 16384
  21.7 0.1 copy-done.2
  21.8 0.0 copy-start.1
  21.8 0.6 %copy.18 = f32[1,2048]{1,0:T(1,128)} copy(f32[1,2048]{1,0:T(1,128)S(1)} %bitcast.23) | data formatting | bytes 16384
  22.4 0.1 copy-done.1
  22.5 0.0 copy-start
  22.5 0.6 %copy.19 = f32[1,2048]{1,0:T(1,128)} copy(f32[1,2048]{1,0:T(1,128)S(1)} %bitcast.22) | data formatting | bytes 16384
  23.1 0.1 copy-done
  23.2 0.6 %copy.20 = f32[1,2048]{1,0:T(1,128)} copy(f32[1,2048]{1,0:T(1,128)S(1)} %bitcast.21) | data formatting | bytes 16384
Async XLA Ops:
  19.2 0.7 %copy-start.4 = (f32[1,128]{1,0:T(1,128)S(1)}, f32[1,128]{1,0:T(1,128)}, u32[]{:S(2)}) copy-start(f32[1,128]{1,0:T(1,128)} %get-tuple-element.17) | copy-start | bytes 1540
  20.4 0.7 %copy-start.3 = (f32[16,128]{1,0:T(8,128)S(1)}, f32[16,128]{1,0:T(8,128)}, u32[]{:S(2)}) copy-start(f32[16,128]{1,0:T(8,128)} %get-tuple-element.13) | copy-start | bytes 24580
  21.1 0.7 %copy-start.2 = (f32[16,128]{1,0:T(8,128)S(1)}, f32[16,128]{1,0:T(8,128)}, u32[]{:S(2)}) copy-start(f32[16,128]{1,0:T(8,128)} %get-tuple-element.14) | copy-start | bytes 24580
  21.8 0.7 %copy-start.1 = (f32[16,128]{1,0:T(8,128)S(1)}, f32[16,128]{1,0:T(8,128)}, u32[]{:S(2)}) copy-start(f32[16,128]{1,0:T(8,128)} %get-tuple-element.15) | copy-start | bytes 24580
  22.5 0.7 %copy-start = (f32[16,128]{1,0:T(8,128)S(1)}, f32[16,128]{1,0:T(8,128)}, u32[]{:S(2)}) copy-start(f32[16,128]{1,0:T(8,128)} %get-tuple-element.16) | copy-start | bytes 24580

commit v2 on v1

--- a/solution.py
+++ b/solution.py
@@ -14,7 +14,7 @@
 
 
 def kernel(n_dp, n_rep, grad_hbm, master_hbm, moment_hbm, second_hbm,
-           row_out, master_out, moment_out, second_out, dir_out, ratio_out,
+           row_out, blocks_out, ratio_out,
            raw, state, tiles, rows_out, rows_in, parts, full, stats,
            load_sem, state_send, state_recv, row_send, row_recv,
            part_send, part_recv, stat_send, stat_recv):
@@ -111,8 +111,8 @@
     row_out[...] = new_master
     for i, value in enumerate((new_master, new_moment, new_second, direction)):
         full[i] = value
-    for i, out in enumerate((master_out, moment_out, second_out, dir_out)):
-        out[...] = full[i, own]
+    for i in range(4):
+        blocks_out[i] = full[i, own]
 
     for copy in stat_copies:
         copy.wait_recv()
@@ -132,6 +132,14 @@
         copy.wait_send()
 
 
+def finish(row_ref, blocks_ref, ratio_ref, params_out, master_out, moment_out, second_out, dir_out, ratio_out):
+    for t in range(row_ref.shape[0]):
+        params_out[:, t * LANES:(t + 1) * LANES] = row_ref[t:t + 1, :].astype(jnp.bfloat16)
+    for i, out in enumerate((master_out, moment_out, second_out, dir_out)):
+        out[...] = blocks_ref[i]
+    ratio_out[...] = ratio_ref[0, :MATS]
+
+
 def local(gradient, master, moment, second):
     raw_rows = gradient[0, 0]
     rows, width = raw_rows.shape
@@ -143,13 +151,15 @@
     vmem = pl.BlockSpec(memory_space=pltpu.VMEM)
     dma = pltpu.SemaphoreType.DMA
     flat = [a.reshape(block, LANES) for a in (master, moment, second)]
-    outs = pl.pallas_call(
+    row, blocks, ratios = pl.pallas_call(
         functools.partial(kernel, n_dp, n_rep),
-        out_shape=[jax.ShapeDtypeStruct((length, LANES), f32)]
-        + [jax.ShapeDtypeStruct((block, LANES), f32)] * 4
-        + [jax.ShapeDtypeStruct((1, LANES), f32)],
+        out_shape=[
+            pltpu.VMEM((length, LANES), f32),
+            pltpu.VMEM((4, block, LANES), f32),
+            pltpu.VMEM((1, LANES), f32),
+        ],
         in_specs=[pl.BlockSpec(memory_space=pl.ANY)] * 4,
-        out_specs=[vmem] * 6,
+        out_specs=[vmem] * 3,
         scratch_shapes=[
             pltpu.VMEM((rows, width), jnp.bfloat16),
             pltpu.VMEM((3, length, LANES), f32),
@@ -167,10 +177,19 @@
         ],
         compiler_params=pltpu.CompilerParams(collective_id=0, has_side_effects=True),
     )(raw_rows, *flat)
-    row, new_master, new_moment, new_second, direction, ratios = outs
-    new_params = row.reshape(1, width).astype(jnp.bfloat16)
-    blocks = [a.reshape(1, cols) for a in (new_master, new_moment, new_second, direction)]
-    return (new_params, *blocks, ratios[0, :MATS])
+    row, blocks, ratios = (
+        pltpu.with_memory_space_constraint(a, pltpu.VMEM) for a in (row, blocks, ratios))
+    outs = pl.pallas_call(
+        finish,
+        out_shape=[jax.ShapeDtypeStruct((1, width), jnp.bfloat16)]
+        + [jax.ShapeDtypeStruct((block, LANES), f32)] * 4
+        + [jax.ShapeDtypeStruct((MATS,), f32)],
+        in_specs=[vmem] * 3,
+        out_specs=[vmem] * 6,
+    )(row, blocks, ratios)
+    new_params, new_master, new_moment, new_second, direction, ratios = outs
+    new_blocks = [a.reshape(1, cols) for a in (new_master, new_moment, new_second, direction)]
+    return (new_params, *new_blocks, ratios)
 
 
 def solution(mesh):

time: 24.2 us -> 18.6 us (0.77); the launches traced: 23.8 us -> 18.5 us
  local copies, waits for them, and re-layouts: 4.57 us -> 0 us
  other arithmetic: 0.76 us -> 0 us
    unnamed x15 -> x0, local copies, waits for them, and re-layouts: 4.06 us -> none
    unnamed x1 -> x0, other arithmetic: 0.76 us -> none
    squeeze x1 -> x0, local copies, waits for them, and re-layouts: 0.51 us -> none  [local(): return (new_params, *blocks, ratios[0, :MATS])]
    pallas_call x1 -> x2, Pallas kernels: 17.8 us -> 17.8 us  [the longest x1 17.2 us: local(): pl.pallas_call(functools.partial(kernel, n_dp, n_rep), out_shape=[pltpu.V...]
where the time goes in v2:
time: 18.6 us; the launch traced here: 18.5 us
  Pallas kernels  17.8 us (96%)
  between operations  0.64 us (3%)
    pallas_call x1, Pallas kernels, local(): pl.pallas_call(functools.partial(kernel, n_dp, n_rep), out_shape=[pltpu.V...  17.2 us
    pallas_call x1, Pallas kernels, local(): pl.pallas_call(finish, out_shape=[jax.ShapeDtypeStruct((1, width), jnp.bf...  0.67 us

profile of v2, /device:TPU:0, one launch (start us, length us, event | category | flops | bytes accessed | tf_op | source)
XLA Modules:
  0.0 18.5 jit_solution(2493780907167436134)
XLA Ops:
  0.6 17.2 %shard_map.91 = (f32[64,128]{1,0:T(8,128)S(1)}, f32[4,16,128]{2,1,0:T(8,128)S(1)}, f32[1,128]{1,0:T(1,128)S(1)}) custom-call(bf16[8,8192]{1,0:T(8,128)(2,1)} %bitcast.8, f32[16,128]{1,0:T(8,128)} %bitcast.9, f32[16,128]{1,0:T(8,128)} %bitcast.10, f32[16,128]{1,0:T(8,128)} %bitcast.11), custom_call_target="tpu_custom_call" | custom-call | tf_op jit(solution)/shard_map/pallas_call | solution.py:154
  17.8 0.7 %shard_map.92 = (bf16[1,8192]{1,0:T(2,128)(2,1)}, f32[16,128]{1,0:T(8,128)}, f32[16,128]{1,0:T(8,128)}, f32[16,128]{1,0:T(8,128)}, f32[16,128]{1,0:T(8,128)}, /*index=5*/f32[4]{0:T(128)}) custom-call(f32[64,128]{1,0:T(8,128)S(1)} %get-tuple-element.15.row_ref, f32[4,16,128]{2,1,0:T(8,128)S(1)} %get-tuple-element.16.blocks_ref, ...), custom_call_target="tpu_custom_call" | custom-call | tf_op jit(solution)/shard_map/pallas_call | solution.py:182

commit v3 on v2

--- a/solution.py
+++ b/solution.py
@@ -13,7 +13,7 @@
 IDS = pl.DeviceIdType.MESH
 
 
-def kernel(n_dp, n_rep, grad_hbm, master_hbm, moment_hbm, second_hbm,
+def staged(n_dp, n_rep, grad_hbm, master_hbm, moment_hbm, second_hbm,
            row_out, blocks_out, ratio_out,
            raw, state, tiles, rows_out, rows_in, parts, full, stats,
            load_sem, state_send, state_recv, row_send, row_recv,
@@ -132,6 +132,118 @@
         copy.wait_send()
 
 
+def direct(n_dp, n_rep, grad_hbm, master_hbm, moment_hbm, second_hbm,
+           row_out, blocks_out, ratio_out,
+           raw, state, tiles, outgoing, incoming, params, stat, stats,
+           load_sem, row_send, row_recv, param_send, param_recv, stat_send, stat_recv):
+    dp = lax.axis_index("dp")
+    rep = lax.axis_index("replica")
+    rows, cols = raw.shape[1:]
+    block = cols // LANES
+    peers = [(j, k) for j in list(range(1, n_rep)) + [0] for k in range(n_dp) if j or k]
+    count = len(peers)
+
+    def at(j, k):
+        return {"dp": lax.rem(dp + k, n_dp), "replica": lax.rem(rep + j, n_rep)}
+
+    def remote(src, dst, send, recv, peer):
+        return pltpu.make_async_remote_copy(
+            src_ref=src, dst_ref=dst, send_sem=send, recv_sem=recv,
+            device_id=peer, device_id_type=IDS)
+
+    loads = {}
+    for j in list(range(1, n_rep)) + [0]:
+        first = pl.multiple_of(lax.rem(rep + j, n_rep) * cols, cols)
+        loads[j] = pltpu.make_async_copy(grad_hbm.at[:, pl.ds(first, cols)], raw.at[j], load_sem.at[j])
+        loads[j].start()
+    state_loads = [
+        pltpu.make_async_copy(ref, state.at[i], load_sem.at[n_rep + i])
+        for i, ref in enumerate((master_hbm, moment_hbm, second_hbm))
+    ]
+    for load in state_loads:
+        load.start()
+
+    barrier = pltpu.get_barrier_semaphore()
+    for j, k in peers:
+        pl.semaphore_signal(barrier, inc=1, device_id=at(j, k), device_id_type=IDS)
+
+    slot = 0
+    row_copies = []
+    for j in list(range(1, n_rep)) + [0]:
+        loads[j].wait()
+        for t in range(block):
+            tile = raw[j, :, t * LANES:(t + 1) * LANES].astype(jnp.float32)
+            tiles[j, t * rows:(t + 1) * rows, :] = tile
+        if slot == 0:
+            pl.semaphore_wait(barrier, count)
+        for k in range(n_dp):
+            if j == 0 and k == 0:
+                continue
+            target = lax.rem(dp + k, n_dp)
+            outgoing[slot] = tiles[j, pl.ds(target, block, stride=rows), :].astype(jnp.bfloat16)
+            copy = remote(outgoing.at[slot], incoming.at[slot], row_send.at[slot], row_recv.at[slot], at(j, k))
+            copy.start()
+            row_copies.append(copy)
+            slot += 1
+
+    for load in state_loads:
+        load.wait()
+    master = state[0]
+    wgt_sq = jnp.sum(master * master, axis=0, keepdims=True)
+    stat[1:2] = wgt_sq
+    total = tiles[0, pl.ds(dp, block, stride=rows), :]
+    for s in range(count):
+        row_copies[s].wait_recv()
+        total = total + incoming[s].astype(jnp.float32)
+    grad = total * (1.0 / (n_dp * n_rep))
+    new_moment = 0.9 * state[1] + 0.1 * grad
+    new_second = 0.999 * state[2] + 0.001 * grad * grad
+    first_scale = 1.0 / (1.0 - 0.9**STEP)
+    second_scale = 1.0 / (1.0 - 0.999**STEP)
+    direction = new_moment * first_scale / (jnp.sqrt(new_second * second_scale) + 1e-08)
+    new_master = master - 0.0003 * (direction + 0.1 * master)
+
+    stat[0:1] = jnp.sum(direction * direction, axis=0, keepdims=True)
+    mine = dp * n_rep + rep
+    stat_copies = []
+    for s, (j, k) in enumerate(peers):
+        copy = remote(stat, stats.at[mine], stat_send.at[s], stat_recv.at[s], at(j, k))
+        copy.start()
+        stat_copies.append(copy)
+    params[rep] = new_master.astype(jnp.bfloat16)
+    param_copies = []
+    for j in range(1, n_rep):
+        copy = remote(params.at[rep], params.at[rep], param_send.at[j], param_recv.at[j], at(j, 0))
+        copy.start()
+        param_copies.append(copy)
+
+    stats[mine] = stat[...]
+    for i, value in enumerate((new_master, new_moment, new_second, direction)):
+        blocks_out[i] = value
+    for copy in row_copies:
+        copy.wait_send()
+
+    for copy in param_copies:
+        copy.wait_recv()
+    for r in range(n_rep):
+        row_out[r * block:(r + 1) * block, :] = params[r].astype(jnp.float32)
+    for copy in stat_copies:
+        copy.wait_recv()
+    per_mat = n_dp * n_rep // MATS
+    lane = lax.broadcasted_iota(jnp.int32, (1, LANES), 1)
+    ratios = jnp.zeros((1, LANES), jnp.float32)
+    for m in range(MATS):
+        pair = stats[m * per_mat]
+        for r in range(1, per_mat):
+            pair = pair + stats[m * per_mat + r]
+        norms = jnp.sqrt(jnp.sum(pair, axis=1, keepdims=True))
+        ratio = norms[0:1] / (norms[1:2] + 1e-06)
+        ratios = jnp.where(lane == m, ratio, ratios)
+    ratio_out[...] = ratios
+    for copy in param_copies + stat_copies:
+        copy.wait_send()
+
+
 def finish(row_ref, blocks_ref, ratio_ref, params_out, master_out, moment_out, second_out, dir_out, ratio_out):
     for t in range(row_ref.shape[0]):
         params_out[:, t * LANES:(t + 1) * LANES] = row_ref[t:t + 1, :].astype(jnp.bfloat16)
@@ -151,16 +263,26 @@
     vmem = pl.BlockSpec(memory_space=pltpu.VMEM)
     dma = pltpu.SemaphoreType.DMA
     flat = [a.reshape(block, LANES) for a in (master, moment, second)]
-    row, blocks, ratios = pl.pallas_call(
-        functools.partial(kernel, n_dp, n_rep),
-        out_shape=[
-            pltpu.VMEM((length, LANES), f32),
-            pltpu.VMEM((4, block, LANES), f32),
-            pltpu.VMEM((1, LANES), f32),
-        ],
-        in_specs=[pl.BlockSpec(memory_space=pl.ANY)] * 4,
-        out_specs=[vmem] * 3,
-        scratch_shapes=[
+    count = n_dp * n_rep
+    if count <= 64:
+        body = direct
+        scratch = [
+            pltpu.VMEM((n_rep, rows, cols), jnp.bfloat16),
+            pltpu.VMEM((3, block, LANES), f32),
+            pltpu.VMEM((n_rep, rows * block, LANES), f32),
+            pltpu.VMEM((count - 1, block, LANES), jnp.bfloat16),
+            pltpu.VMEM((count - 1, block, LANES), jnp.bfloat16),
+            pltpu.VMEM((n_rep, block, LANES), jnp.bfloat16),
+            pltpu.VMEM((2, LANES), f32),
+            pltpu.VMEM((count, 2, LANES), f32),
+            dma((n_rep + 3,)),
+            dma((count - 1,)), dma((count - 1,)),
+            dma((n_rep,)), dma((n_rep,)),
+            dma((count - 1,)), dma((count - 1,)),
+        ]
+    else:
+        body = staged
+        scratch = [
             pltpu.VMEM((rows, width), jnp.bfloat16),
             pltpu.VMEM((3, length, LANES), f32),
             pltpu.VMEM((rows * length, LANES), f32),
@@ -174,7 +296,17 @@
             dma((n_dp,)), dma((n_dp,)),
             dma((n_rep,)), dma((n_rep,)),
             dma((n_dp,)), dma((n_dp,)),
+        ]
+    row, blocks, ratios = pl.pallas_call(
+        functools.partial(body, n_dp, n_rep),
+        out_shape=[
+            pltpu.VMEM((length, LANES), f32),
+            pltpu.VMEM((4, block, LANES), f32),
+            pltpu.VMEM((1, LANES), f32),
         ],
+        in_specs=[pl.BlockSpec(memory_space=pl.ANY)] * 4,
+        out_specs=[vmem] * 3,
+        scratch_shapes=scratch,
         compiler_params=pltpu.CompilerParams(collective_id=0, has_side_effects=True),
     )(raw_rows, *flat)
     row, blocks, ratios = (

time: 18.6 us -> 20.3 us (1.091)
  Pallas kernels: 17.8 us -> 19.5 us
    pallas_call x1, Pallas kernels: 17.2 us -> 18.8 us  [local(): pl.pallas_call(functools.partial(body, n_dp, n_rep), out_shape=[pltpu.VME...]
where the time goes in v3:
time: 20.3 us; the launch traced here: 20.1 us
  Pallas kernels  19.5 us (96%)
  between operations  0.64 us (3%)
    pallas_call x1, Pallas kernels, local(): pl.pallas_call(functools.partial(body, n_dp, n_rep), out_shape=[pltpu.VME...  18.8 us
    pallas_call x1, Pallas kernels, local(): pl.pallas_call(finish, out_shape=[jax.ShapeDtypeStruct((1, width), jnp.bf...  0.67 us

profile of v3, /device:TPU:0, one launch (start us, length us, event | category | flops | bytes accessed | tf_op | source)
XLA Modules:
  0.0 20.1 jit_solution(8669420050187330738)
XLA Ops:
  0.6 18.8 %shard_map.91 = (f32[64,128]{1,0:T(8,128)S(1)}, f32[4,16,128]{2,1,0:T(8,128)S(1)}, f32[1,128]{1,0:T(1,128)S(1)}) custom-call(bf16[8,8192]{1,0:T(8,128)(2,1)} %bitcast.8, f32[16,128]{1,0:T(8,128)} %bitcast.9, f32[16,128]{1,0:T(8,128)} %bitcast.10, f32[16,128]{1,0:T(8,128)} %bitcast.11), custom_call_target="tpu_custom_call" | custom-call | tf_op jit(solution)/shard_map/pallas_call | solution.py:300
  19.5 0.7 %shard_map.92 = (bf16[1,8192]{1,0:T(2,128)(2,1)}, f32[16,128]{1,0:T(8,128)}, f32[16,128]{1,0:T(8,128)}, f32[16,128]{1,0:T(8,128)}, f32[16,128]{1,0:T(8,128)}, /*index=5*/f32[4]{0:T(128)}) custom-call(f32[64,128]{1,0:T(8,128)S(1)} %get-tuple-element.15.row_ref, f32[4,16,128]{2,1,0:T(8,128)S(1)} %get-tuple-element.16.blocks_ref, ...), custom_call_target="tpu_custom_call" | custom-call | tf_op jit(solution)/shard_map/pallas_call | solution.py:314

commit v4 on v2

--- a/solution.py
+++ b/solution.py
@@ -35,77 +35,74 @@
             src_ref=src, dst_ref=dst, send_sem=send, recv_sem=recv,
             device_id=peer, device_id_type=IDS)
 
+    def settle(ref, sem):
+        pltpu.make_async_copy(ref, ref, sem.at[0]).wait()
+
     own = pl.ds(pl.multiple_of(rep * block, block), block)
+    offsets = sorted(range(1, n_dp), key=lambda k: abs(2 * k - n_dp))
     grad_load = pltpu.make_async_copy(grad_hbm, raw, load_sem.at[0])
     grad_load.start()
+
+    barrier = pltpu.get_barrier_semaphore()
+    for k in offsets:
+        pl.semaphore_signal(barrier, inc=1, device_id=dp_peer(k), device_id_type=IDS)
+    for k in range(1, n_rep):
+        pl.semaphore_signal(barrier, inc=1, device_id=rep_peer(k), device_id_type=IDS)
+
     state_loads = [
         pltpu.make_async_copy(ref, state.at[i, own], load_sem.at[1 + i])
         for i, ref in enumerate((master_hbm, moment_hbm, second_hbm))
     ]
     for load in state_loads:
         load.start()
-
-    barrier = pltpu.get_barrier_semaphore()
-    for k in range(1, n_dp):
-        pl.semaphore_signal(barrier, inc=1, device_id=dp_peer(k), device_id_type=IDS)
-    for k in range(1, n_rep):
-        pl.semaphore_signal(barrier, inc=1, device_id=rep_peer(k), device_id_type=IDS)
-
     grad_load.wait()
     for t in range(length):
         tile = raw[:, t * LANES:(t + 1) * LANES].astype(jnp.float32)
         tiles[t * rows:(t + 1) * rows, :] = tile
-    pl.semaphore_wait(barrier, n_dp + n_rep - 2)
-
-    row_copies = []
-    for k in range(1, n_dp):
+    for k in offsets:
         peer = lax.rem(dp + k, n_dp)
         rows_out[k] = tiles[pl.ds(peer, length, stride=rows), :].astype(jnp.bfloat16)
-        copy = remote(rows_out.at[k], rows_in.at[k], row_send.at[k], row_recv.at[k], dp_peer(k))
-        copy.start()
-        row_copies.append(copy)
-
     for load in state_loads:
         load.wait()
-    state_copies = []
+    pl.semaphore_wait(barrier, n_dp + n_rep - 2)
+
+    for k in offsets:
+        copy = remote(rows_out.at[k], rows_in.at[k], row_send.at[0], row_recv.at[0], dp_peer(k))
+        copy.start()
     for k in range(1, n_rep):
-        copy = remote(state.at[:, own], state.at[:, own], state_send.at[k], state_recv.at[k], rep_peer(k))
-        copy.start()
-        state_copies.append(copy)
+        copy = remote(state.at[:, own], state.at[:, own], state_send.at[0], state_recv.at[0], rep_peer(k))
+        copy.start()
 
     total = tiles[pl.ds(dp, length, stride=rows), :]
-    for k in range(1, n_dp):
-        row_copies[k - 1].wait_recv()
+    settle(rows_in.at[1:n_dp], row_recv)
+    for k in offsets:
         total = total + rows_in[k].astype(jnp.float32)
     parts[rep] = total
-    part_copies = []
     for k in range(1, n_rep):
-        copy = remote(parts.at[rep], parts.at[rep], part_send.at[k], part_recv.at[k], rep_peer(k))
-        copy.start()
-        part_copies.append(copy)
-
-    for copy in state_copies:
-        copy.wait_recv()
-    for copy in part_copies:
-        copy.wait_recv()
+        copy = remote(parts.at[rep], parts.at[rep], part_send.at[0], part_recv.at[0], rep_peer(k))
+        copy.start()
+
+    settle(state.at[:, 0:(n_rep - 1) * block], state_recv)
+    master = state[0]
+    stats[dp, 1:2] = jnp.sum(master * master, axis=0, keepdims=True)
+    old_moment = 0.9 * state[1]
+    old_second = 0.999 * state[2]
+    settle(rows_out.at[1:n_dp], row_send)
+    settle(state.at[:, 0:(n_rep - 1) * block], state_send)
+    settle(parts.at[1:n_rep], part_recv)
     summed = parts[0]
     for r in range(1, n_rep):
         summed = summed + parts[r]
-    grad = summed / (n_dp * n_rep)
-    master = state[0]
-    new_moment = 0.9 * state[1] + 0.1 * grad
-    new_second = 0.999 * state[2] + 0.001 * grad * grad
-    first_fix = 1.0 - 0.9**STEP
-    second_fix = 1.0 - 0.999**STEP
-    direction = new_moment / first_fix / (jnp.sqrt(new_second / second_fix) + 1e-08)
-    dir_sq = jnp.sum(direction * direction, axis=0, keepdims=True)
-    wgt_sq = jnp.sum(master * master, axis=0, keepdims=True)
-    stats[dp] = jnp.concatenate([dir_sq, wgt_sq], axis=0)
-    stat_copies = []
-    for k in range(1, n_dp):
-        copy = remote(stats.at[dp], stats.at[dp], stat_send.at[k], stat_recv.at[k], dp_peer(k))
-        copy.start()
-        stat_copies.append(copy)
+    grad = summed * (1.0 / (n_dp * n_rep))
+    new_moment = old_moment + 0.1 * grad
+    new_second = old_second + 0.001 * grad * grad
+    first_scale = 1.0 / (1.0 - 0.9**STEP)
+    second_scale = 1.0 / (1.0 - 0.999**STEP)
+    direction = new_moment * first_scale / (jnp.sqrt(new_second * second_scale) + 1e-08)
+    stats[dp, 0:1] = jnp.sum(direction * direction, axis=0, keepdims=True)
+    for k in offsets:
+        copy = remote(stats.at[dp], stats.at[dp], stat_send.at[0], stat_recv.at[0], dp_peer(k))
+        copy.start()
 
     new_master = master - 0.0003 * (direction + 0.1 * master)
     row_out[...] = new_master
@@ -113,9 +110,9 @@
         full[i] = value
     for i in range(4):
         blocks_out[i] = full[i, own]
-
-    for copy in stat_copies:
-        copy.wait_recv()
+    settle(parts.at[1:n_rep], part_send)
+
+    settle(stats.at[1:n_dp], stat_recv)
     per_mat = rows // MATS
     lane = lax.broadcasted_iota(jnp.int32, (1, LANES), 1)
     ratios = jnp.zeros((1, LANES), jnp.float32)
@@ -128,8 +125,7 @@
         ratios = jnp.where(lane == m, ratio, ratios)
     ratio_out[...] = ratios
 
-    for copy in row_copies + state_copies + part_copies + stat_copies:
-        copy.wait_send()
+    settle(stats.at[1:n_dp], stat_send)
 
 
 def finish(row_ref, blocks_ref, ratio_ref, params_out, master_out, moment_out, second_out, dir_out, ratio_out):
@@ -170,10 +166,7 @@
             pltpu.VMEM((4, length, LANES), f32),
             pltpu.VMEM((n_dp, 2, LANES), f32),
             dma((4,)),
-            dma((n_rep,)), dma((n_rep,)),
-            dma((n_dp,)), dma((n_dp,)),
-            dma((n_rep,)), dma((n_rep,)),
-            dma((n_dp,)), dma((n_dp,)),
+            *[dma((1,))] * 8,
         ],
         compiler_params=pltpu.CompilerParams(collective_id=0, has_side_effects=True),
     )(raw_rows, *flat)

time: 18.6 us -> 18.2 us (0.978)
  Pallas kernels: 17.8 us -> 17.4 us
    pallas_call x1, Pallas kernels: 17.2 us -> 16.8 us  [local(): pl.pallas_call(functools.partial(kernel, n_dp, n_rep), out_shape=[pltpu.V...]
where the time goes in v4:
time: 18.2 us; the launch traced here: 18.1 us
  Pallas kernels  17.4 us (96%)
  between operations  0.64 us (4%)
    pallas_call x1, Pallas kernels, local(): pl.pallas_call(functools.partial(kernel, n_dp, n_rep), out_shape=[pltpu.V...  16.8 us
    pallas_call x1, Pallas kernels, local(): pl.pallas_call(finish, out_shape=[jax.ShapeDtypeStruct((1, width), jnp.bf...  0.67 us

profile of v4, /device:TPU:0, one launch (start us, length us, event | category | flops | bytes accessed | tf_op | source)
XLA Modules:
  0.0 18.1 jit_solution(283305268065581775)
XLA Ops:
  0.6 16.8 %shard_map.91 = (f32[64,128]{1,0:T(8,128)S(1)}, f32[4,16,128]{2,1,0:T(8,128)S(1)}, f32[1,128]{1,0:T(1,128)S(1)}) custom-call(bf16[8,8192]{1,0:T(8,128)(2,1)} %bitcast.8, f32[16,128]{1,0:T(8,128)} %bitcast.9, f32[16,128]{1,0:T(8,128)} %bitcast.10, f32[16,128]{1,0:T(8,128)} %bitcast.11), custom_call_target="tpu_custom_call" | custom-call | tf_op jit(solution)/shard_map/pallas_call | solution.py:150
  17.4 0.7 %shard_map.92 = (bf16[1,8192]{1,0:T(2,128)(2,1)}, f32[16,128]{1,0:T(8,128)}, f32[16,128]{1,0:T(8,128)}, f32[16,128]{1,0:T(8,128)}, f32[16,128]{1,0:T(8,128)}, /*index=5*/f32[4]{0:T(128)}) custom-call(f32[64,128]{1,0:T(8,128)S(1)} %get-tuple-element.15.row_ref, f32[4,16,128]{2,1,0:T(8,128)S(1)} %get-tuple-element.16.blocks_ref, ...), custom_call_target="tpu_custom_call" | custom-call | tf_op jit(solution)/shard_map/pallas_call | solution.py:175
